TPU v7x, 32 devices: a whole 2x2x4 slice. The times are simulated.
32 devices in a mesh: lon: 8 (over z, core), mem: 4 (over y, x).
Axes of the slice: x: 2, y: 2, z: 4, core: 2. Of those that a mesh axis runs over, the one named last changes fastest.
Arguments:
- members: float32 [32, 4, 192, 256], P('mem', None, 'lon'), may hold values from -6 to 6
- courant_lon: float32 [4, 192, 256], P(None, 'lon'), may hold values from -0.55 to 0.55
- courant_lat: float32 [4, 192, 256], P(None, 'lon'), may hold values from -0.4 to 0.4
- vert_modes: float32 [2, 4], replicated, may hold values from -1 to 1
- horiz_modes: float32 [4, 192, 256], P(None, 'lon'), may hold values from -1 to 1
- obs_index: int32 [16384], P('lon'), may hold values from 0 to 24575
- obs_count: int32 [8], P('lon'), may hold values from 1024 to 2048, as said below
- obs_value: float32 [16384], P('lon'), may hold values from -6 to 6
- obs_var: float32 [16384], P('lon'), may hold values from 2 to 48
Outputs:
- prior_trajectories: float32 [32, 4, 192, 256], P('mem', None, 'lon')
- analysis_mean: float32 [4, 192, 256], P(None, 'lon')
Inputs may be any that keep to these rules, and one draw needn't show every extreme that they name: `obs_index`: index of a cell within the band's own block: level, then longitude within the band, then latitude. Each band uses its first obs_count slots; some band uses all 2048.
All inputs are finite; a program needn't handle non-finite values.
Results may differ from a plain program's by a relative error of at most 0.0001.
Values sent between devices are 32-bit elements; how exact they have to be, the bound alone decides.
A program may use at most 128 MiB of HBM per device.

v0:
```python
import jax
import jax.numpy as jnp
from jax import lax
from jax.sharding import PartitionSpec as P

KV = 2
KH = 4
ADV_STEPS = 2


def padded(block, sides, width):
    for axis, dim in sides:
        count = lax.axis_size(axis)
        forward = [(i, i + 1) for i in range(count - 1)]
        forward.append((count - 1, 0))
        backward = [(target, source) for source, target in forward]
        low = lax.ppermute(
            lax.slice_in_dim(block, block.shape[dim] - width, None, axis=dim), axis, forward
        )
        high = lax.ppermute(lax.slice_in_dim(block, 0, width, axis=dim), axis, backward)
        block = jnp.concatenate([low, block, high], axis=dim)
    return block


def update(centre, western, eastern, flow_lon, flow_lat):
    zero_col = jnp.zeros_like(centre[..., :1])
    south_boundary = jnp.concatenate([zero_col, centre[..., :-1]], axis=-1)
    northern = jnp.concatenate([centre[..., 1:], zero_col], axis=-1)
    result = centre - jnp.maximum(flow_lon, 0.0) * (centre - western)
    result = result - jnp.minimum(flow_lon, 0.0) * (eastern - centre)
    result = result - jnp.maximum(flow_lat, 0.0) * (centre - south_boundary)
    result = result - jnp.minimum(flow_lat, 0.0) * (northern - centre)
    return result


def per_device(
    members,
    courant_lon,
    courant_lat,
    vert_modes,
    horiz_modes,
    obs_index,
    obs_count,
    obs_value,
    obs_var,
):
    mem_dev, layer_tally, band_width, lat_rows = members.shape
    sample_tally_overall = mem_dev * lax.axis_size("mem")
    rim_depth = ADV_STEPS
    stacked = jnp.concatenate(
        [members.reshape(mem_dev * layer_tally, band_width, lat_rows), courant_lon, courant_lat],
        axis=0,
    )
    extended = padded(stacked, (("lon", 1),), rim_depth)
    split_at = mem_dev * layer_tally
    prognostic_vector = extended[:split_at].reshape(
        mem_dev, layer_tally, band_width + 2 * rim_depth, lat_rows
    )
    flow_lon_ext = extended[split_at : split_at + layer_tally]
    meridional_wind_padded = extended[split_at + layer_tally :]
    for section in range(rim_depth):
        out_cols = band_width + 2 * (rim_depth - 1 - section)
        first_col = section + 1
        prognostic_vector = update(
            prognostic_vector[:, :, 1 : out_cols + 1],
            prognostic_vector[:, :, 0:out_cols],
            prognostic_vector[:, :, 2 : out_cols + 2],
            flow_lon_ext[:, first_col : first_col + out_cols],
            meridional_wind_padded[:, first_col : first_col + out_cols],
        )
    sample_centroid = lax.psum(jnp.sum(prognostic_vector, axis=0), "mem") / sample_tally_overall
    sample_departure = prognostic_vector - sample_centroid[None]
    norm_scale = (sample_tally_overall - 1) ** (-0.5)
    obs_slots = obs_index.shape[0]
    band_cells = band_width * lat_rows
    level_idx = obs_index // band_cells
    within = obs_index % band_cells
    anomaly_obs = jnp.take(sample_departure.reshape(mem_dev, -1), obs_index, axis=1)
    mean_obs = jnp.take(sample_centroid.reshape(-1), obs_index)
    vert_obs = jnp.take(vert_modes, level_idx, axis=1)
    horiz_obs = jnp.take(horiz_modes.reshape(KH, -1), within, axis=1)
    modes_obs = (vert_obs[:, None, :] * horiz_obs[None, :, :]).reshape(KV * KH, obs_slots)
    live_mask = (jnp.arange(obs_slots, dtype=jnp.int32) < obs_count[0]).astype(jnp.float32)
    obs_perts = (
        anomaly_obs[:, None, :] * modes_obs[None, :, :] * (live_mask * norm_scale)[None, None, :]
    )
    obs_perts = obs_perts.reshape(mem_dev * KV * KH, obs_slots)
    inv_var = live_mask / obs_var
    innovation = obs_value - mean_obs
    all_perts = lax.all_gather(obs_perts, "mem", axis=0, tiled=True)
    gram_part = jnp.dot(all_perts * inv_var[None, :], all_perts.T, precision=lax.Precision.HIGHEST)
    side_part = jnp.dot(all_perts, inv_var * innovation, precision=lax.Precision.HIGHEST)
    gram_matrix, right_side = lax.psum((gram_part, side_part), "lon")
    system = jnp.eye(gram_matrix.shape[0], dtype=jnp.float32) + gram_matrix
    factor = jnp.linalg.cholesky(system)
    weights = jax.scipy.linalg.cho_solve((factor, True), right_side)
    w_mat = weights.reshape(sample_tally_overall, KV * KH)
    w_local = lax.dynamic_slice_in_dim(w_mat, lax.axis_index("mem") * mem_dev, mem_dev, 0)
    mode_coef = jnp.einsum(
        "mk,mlij->klij", w_local, sample_departure, precision=lax.Precision.HIGHEST
    )
    mode_coef = mode_coef.reshape(KV, KH, layer_tally, band_width, lat_rows)
    inc_part = (
        jnp.einsum(
            "al,bij,ablij->lij", vert_modes, horiz_modes, mode_coef, precision=lax.Precision.HIGHEST
        )
        * norm_scale
    )
    posterior_adjustment = lax.psum(inc_part, "mem")
    return (prognostic_vector, sample_centroid + posterior_adjustment)


def solution(mesh):
    placed = (
        P("mem", None, "lon", None),
        P(None, "lon", None),
        P(None, "lon", None),
        P(),
        P(None, "lon", None),
        P("lon"),
        P("lon"),
        P("lon"),
        P("lon"),
    )
    return jax.shard_map(
        per_device,
        mesh=mesh,
        in_specs=placed,
        out_specs=(P("mem", None, "lon", None), P(None, "lon", None)),
        check_vma=False,
    )
```

profile of v0, /device:TPU:0, one launch (start us, length us, event | category | flops | bytes accessed | tf_op | source)
XLA Modules:
  0.0 332.7 jit_solution(16638624239704680310)
XLA Ops:
  7.2 1.2 pad_maximum_fusion.5
  8.4 0.5 collective-permute-start
  8.9 4.1 %collective-permute-start.1 = (f32[40,2,256]{2,1,0:T(2,128)S(1)}, f32[40,2,256]{2,1,0:T(2,128)S(1)}, u32[]{:S(2)}, u32[]{:S(2)}) collective-permute-start(f32[40,2,256]{2,1,0:T(2,128)S(1)} %get-tuple-element.36), channel_id=1, source_target_pairs={{4,0},{8,4},{12,8},{16,12},{20,16},{24,20},{28,24},{0,28},{5,1},{9... | collective-permute-start | bytes 245768 | tf_op jit(solution)/shard_map/ppermute | solution.py:20
  13.0 0.7 compare_and_fusion.1
  13.8 0.7 fusion.30
  14.5 0.8 copy.32
  15.2 5.5 %gather_fusion.1 = f32[2048,2]{1,0:T(8,128)S(1)} fusion(f32[2,4]{0,1:T(4,128)S(1)} %copy.32, s32[2048]{0:T(1024)S(1)} %get-tuple-element.46), kind=kCustom, calls=%fused_computation.1 | custom fusion | bytes 40960 | tf_op jit(solution)/shard_map/jit(_take)/gather | solution.py:80
  20.7 0.3 select_bitcast_fusion.1
  21.0 0.3 copy.33
  21.4 2.3 copy.34
  23.6 7.4 %gather_fusion.2 = f32[2048,4]{1,0:T(8,128)S(1)} fusion(f32[4,6144]{0,1:T(8,128)} %bitcast.119, s32[2048]{0:T(1024)S(1)} %get-tuple-element.47), kind=kCustom, calls=%fused_computation.2 | custom fusion | bytes 73728 | tf_op jit(solution)/shard_map/jit(_take)/gather | solution.py:81
  31.1 0.3 select_bitcast_fusion
  31.4 0.3 copy.35
  32.6 0.2 pad_maximum_fusion
  32.8 0.1 slice.157
  32.9 0.4 fusion.43
  33.4 0.7 fusion.9
  34.1 0.3 fusion.42
  34.4 1.2 fusion.39
  35.6 41.8 %all-reduce.9.cloned.1.call-done = f32[4,24,256]{2,1,0:T(8,128)} async-done(((f32[4,24,256]{2,1,0:T(8,128)}), f32[4,24,256]{2,1,0:T(8,128)}) %all-reduce.9.cloned.1.call-update) | async-done | bytes 98320 | tf_op jit(solution)/shard_map/psum | solution.py:71
  77.5 0.9 broadcast_multiply_fusion
  78.5 6.6 %copy.30 = f32[8,4,24,256]{0,3,2,1:T(8,128)} copy(f32[8,4,24,256]{3,2,1,0:T(8,128)S(1)} %broadcast_subtract_fusion) | data formatting | bytes 1572864 | tf_op jit(solution)/shard_map/sub | solution.py:72
  85.1 11.8 %gather_fusion.3 = f32[2048]{0:T(1024)S(1)} fusion(f32[24576]{0:T(1024)S(1)} %bitcast.112, s32[2048]{0:T(1024)S(1)} %get-tuple-element.45), kind=kCustom, calls=%fused_computation.3 | custom fusion | bytes 24576 | tf_op jit(solution)/shard_map/jit(_take)/gather | solution.py:79
  96.9 10.0 %gather_fusion = f32[2048,8]{1,0:T(8,128)S(1)} fusion(f32[8,24576]{0,1:T(8,128)} %bitcast.113, s32[2048]{0:T(1024)S(1)} %get-tuple-element.45), kind=kCustom, calls=%fused_computation | custom fusion | bytes 139264 | tf_op jit(solution)/shard_map/jit(_take)/gather | solution.py:78
  107.0 0.3 select_bitcast_fusion.2
  107.3 0.3 copy.31
  107.6 0.9 bitcast_multiply_fusion
  108.6 0.1 copy.51
  108.8 35.2 %all-gather.2.cloned.1.call-done = f32[256,2048]{1,0:T(8,128)} async-done(((f32[64,2048]{1,0:T(8,128)}), f32[256,2048]{1,0:T(8,128)}) %all-gather.2.cloned.1.call-update) | async-done | bytes 2097168 | tf_op jit(solution)/shard_map/all_gather | solution.py:90
  144.0 5.0 %fusion = f32[256,256]{0,1:T(8,128)} fusion(f32[256,2048]{1,0:T(8,128)} %all-gather.2.cloned.1.call-done, f32[2048]{0:T(1024)S(1)} %get-tuple-element.19), kind=kOutput, calls=%fused_computation.6 | convolution fusion | flops 1611137024 | bytes 2367488 | tf_op jit(solution)/shard_map/dot_general | solution.py:91
  149.1 1.7 fusion.44
  150.8 16.6 %psum.30 = f32[256]{0:T(256)S(1)} all-reduce(f32[256]{0:T(256)S(1)} %bitcast.124), channel_id=1, replica_groups=mesh['lon'=8,'mem'=4] {'lon'}, use_global_device_ids=true, to_apply=%region_7.8 | all-reduce | flops 256 | bytes 2048 | tf_op jit(solution)/shard_map/psum | solution.py:93
  167.4 36.7 %all-reduce.11.cloned.1.call-done = f32[256,256]{0,1:T(8,128)} async-done(((f32[256,256]{0,1:T(8,128)}), f32[256,256]{0,1:T(8,128)}) %all-reduce.11.cloned.1.call-update) | async-done | bytes 262160 | tf_op jit(solution)/shard_map/psum | solution.py:93
  204.1 1.0 convert_add_fusion
  205.1 0.1 copy.37
  205.2 1.0 fusion.19
  206.2 11.7 %cholesky.50 = f32[128,128]{1,0:T(8,128)S(1)} custom-call(f32[128,128]{1,0:T(8,128)S(1)} %cholesky.118), custom_call_target="Cholesky" | custom-call | tf_op jit(solution)/shard_map/jit(cholesky)/cholesky | solution.py:95
  218.0 0.7 compare_reduce_fusion.1
  218.6 9.8 %custom-call.18 = f32[1,128,128]{1,2,0:T(8,128)S(1)} custom-call(f32[1,128,128]{2,1,0:T(8,128)S(1)} %get-tuple-element.44), custom_call_target="InvertDiagBlocksLowerTriangular" | custom-call | tf_op jit(solution)/shard_map/jit(cholesky)/cholesky | solution.py:95
  228.5 0.2 constant_dynamic-update-slice_fusion.1
  228.7 0.3 convolution_subtract_fusion
  229.0 11.7 %cholesky.105 = f32[128,128]{1,0:T(8,128)S(1)} custom-call(f32[128,128]{1,0:T(8,128)S(1)} %convolution_subtract_fusion), custom_call_target="Cholesky" | custom-call | tf_op jit(solution)/shard_map/jit(cholesky)/cholesky | solution.py:95
  240.7 0.6 compare_reduce_fusion
  242.5 0.1 triangular_solve.73
  242.6 3.8 %while.1 = (s32[]{:T(128)}, f32[256,256]{1,0:T(8,128)S(1)}, s32[2,2]{1,0:T(2,128)S(1)}, f32[2,128,128]{2,1,0:T(8,128)S(1)}, s32[]{:T(128)}) while((s32[]{:T(128)}, f32[256,256]{1,0:T(8,128)S(1)}, s32[2,2]{1,0:T(2,128)S(1)}, f32[2,128,128]{2,1,0:T(8,128)S(1)}, s32[]{:T(128)}) %tuple.44), condition=%wide.while_cond, body=%wide.while_body.sunk | while | flops 2 | bytes 131189 | solution.py:96
  242.6 0.6 fusion.57
  243.2 1.3 bitcast_dynamic-update-slice_fusion.2
  244.5 0.6 fusion.57
  245.2 1.3 bitcast_dynamic-update-slice_fusion.2
  246.4 19.9 %custom-call.19 = f32[2,128,128]{1,2,0:T(8,128)S(1)} custom-call(f32[2,128,128]{2,1,0:T(8,128)S(1)} %get-tuple-element.9), custom_call_target="InvertDiagBlocksLowerTriangular" | custom-call | tf_op jit(solution)/shard_map/jit(_cho_solve)/triangular_solve | solution.py:96
  266.3 0.2 fusion.25
  266.5 0.2 fusion.5
  266.7 0.2 convolution_bitcast_fusion.3
  266.9 0.2 convolution_bitcast_fusion.2
  267.1 0.2 fusion.3
  267.3 0.2 convolution_bitcast_fusion
  267.5 0.1 reshape.169
  267.6 13.6 %fusion.31 = f32[8,4,24,256]{3,0,2,1:T(8,128)S(1)} fusion(f32[8,4,24,256]{0,3,2,1:T(8,128)} %copy.30, f32[32,8]{1,0:T(8,128)S(1)} %reshape.169, s32[]{:T(128)S(6)} %select_n.71), kind=kOutput, calls=%fused_computation.98 | convolution fusion | flops 18874368 | bytes 1576964 | tf_op jit(solution)/shard_map/mk,mlij->klij/dot_general | solution.py:99
  281.2 0.2 reshape.170
  281.5 0.6 multiply_reduce_fusion
  282.1 0.8 fusion.20
  283.0 0.7 bitcast_multiply_fusion.1
  283.6 41.0 %all-reduce.13.cloned.1.call-done = f32[4,24,256]{2,1,0:T(8,128)} async-done(((f32[4,24,256]{2,1,0:T(8,128)}), f32[4,24,256]{2,1,0:T(8,128)}) %all-reduce.13.cloned.1.call-update) | async-done | bytes 98320 | tf_op jit(solution)/shard_map/psum | solution.py:109
  324.6 1.5 fusion.38
  (53 shorter events, 0.8 us)
Async XLA Ops:
  7.2 70.3 %all-reduce.9.cloned.1.call-start = ((), (), s32[]{:S(2)}) async-start(), calls=%async_computation | async-start | bytes 196608 | tf_op jit(solution)/shard_map/psum | solution.py:71
  7.2 14.2 %copy-start.5 = (f32[4,24,256]{2,1,0:T(8,128)S(1)}, f32[4,24,256]{2,1,0:T(8,128)}, u32[]{:S(2)}) copy-start(f32[4,24,256]{2,1,0:T(8,128)} %param.13) | copy-start | bytes 294916
  8.4 24.1 %collective-permute-start = (f32[40,2,256]{2,1,0:T(2,128)S(1)}, f32[40,2,256]{2,1,0:T(2,128)S(1)}, u32[]{:S(2)}, u32[]{:S(2)}) collective-permute-start(f32[40,2,256]{2,1,0:T(2,128)S(1)} %get-tuple-element.35), channel_id=1, source_target_pairs={{0,4},{4,8},{8,12},{12,16},{16,20},{20,24},{24,28},{28,0},{1,5},{5... | collective-permute-start | bytes 245768 | tf_op jit(solution)/shard_map/ppermute | solution.py:17
  8.9 23.6 %collective-permute-start.1 = (f32[40,2,256]{2,1,0:T(2,128)S(1)}, f32[40,2,256]{2,1,0:T(2,128)S(1)}, u32[]{:S(2)}, u32[]{:S(2)}) collective-permute-start(f32[40,2,256]{2,1,0:T(2,128)S(1)} %get-tuple-element.36), channel_id=1, source_target_pairs={{4,0},{8,4},{12,8},{16,12},{20,16},{24,20},{28,24},{0,28},{5,1},{9... | collective-permute-start | bytes 245768 | tf_op jit(solution)/shard_map/ppermute | solution.py:20
  23.6 8.2 %copy-start.3 = (f32[4,24,256]{2,1,0:T(8,128)S(1)}, f32[4,24,256]{2,1,0:T(8,128)}, u32[]{:S(2)}) copy-start(f32[4,24,256]{2,1,0:T(8,128)} %param.11) | copy-start | bytes 294916
  23.6 8.2 %copy-start.4 = (f32[4,24,256]{2,1,0:T(8,128)S(1)}, f32[4,24,256]{2,1,0:T(8,128)}, u32[]{:S(2)}) copy-start(f32[4,24,256]{2,1,0:T(8,128)} %param.10) | copy-start | bytes 294916
  23.6 8.9 %copy-start.1 = (f32[8,4,24,256]{3,2,1,0:T(8,128)S(1)}, f32[8,4,24,256]{3,2,1,0:T(8,128)}, u32[]{:S(2)}) copy-start(f32[8,4,24,256]{3,2,1,0:T(8,128)} %param.9) | copy-start | bytes 2359300
  35.6 49.5 %copy-start.2 = (f32[8,4,24,256]{3,2,1,0:T(8,128)}, f32[8,4,24,256]{3,2,1,0:T(8,128)S(1)}, u32[]{:S(2)}) copy-start(f32[8,4,24,256]{3,2,1,0:T(8,128)S(1)} %get-tuple-element.22) | copy-start | bytes 2359300
  35.6 108.4 %all-gather.2.cloned.1.call-start = ((), (), s32[]{:S(2)}) async-start(), calls=%async_computation.1 | async-start | bytes 2621440 | tf_op jit(solution)/shard_map/all_gather | solution.py:90
  85.1 21.8 %copy-start.7 = (s32[2048]{0:T(1024)S(1)}, s32[2048]{0:T(1024)}, u32[]{:S(2)}) copy-start(s32[2048]{0:T(1024)} %param.14) | copy-start | bytes 24580
  85.1 21.9 %copy-start.8 = (f32[2048]{0:T(1024)S(1)}, f32[2048]{0:T(1024)}, u32[]{:S(2)}) copy-start(f32[2048]{0:T(1024)} %param.16) | copy-start | bytes 24580
  85.1 21.9 %copy-start.9 = (f32[2048]{0:T(1024)S(1)}, f32[2048]{0:T(1024)}, u32[]{:S(2)}) copy-start(f32[2048]{0:T(1024)} %param.17) | copy-start | bytes 24580
  107.0 1.6 copy-start.10
  108.5 95.6 %all-reduce.11.cloned.1.call-start = ((), (), s32[]{:S(2)}) async-start(), calls=%async_computation.2 | async-start | bytes 524288 | tf_op jit(solution)/shard_map/psum | solution.py:93
  144.0 5.1 %copy-start = (f32[256,2048]{1,0:T(8,128)S(1)}, f32[256,2048]{1,0:T(8,128)}, u32[]{:S(2)}) copy-start(f32[256,2048]{1,0:T(8,128)} %all-gather.2.cloned.1.call-done) | copy-start | bytes 6291460
  149.0 175.6 %all-reduce.13.cloned.1.call-start = ((), (), s32[]{:S(2)}) async-start(), calls=%async_computation.3 | async-start | bytes 196608 | tf_op jit(solution)/shard_map/psum | solution.py:109
  281.2 43.4 %copy-start.6 = (f32[4,24,256]{2,1,0:T(8,128)S(1)}, f32[4,24,256]{2,1,0:T(8,128)}, u32[]{:S(2)}) copy-start(f32[4,24,256]{2,1,0:T(8,128)} %all-reduce.9.cloned.1.call-done) | copy-start | bytes 294916
Sparse Core Ops, SparseCore 0:
  35.7 41.7 all-reduce.8
  108.6 35.2 all-gather.1
  149.1 54.9 all-reduce.10
  283.8 40.8 all-reduce.12
where the time goes:
time: 333 us
  waiting for transfers between devices  155 us (47%)
  other arithmetic  67 us (20%)
  local copies, waits for them, and re-layouts  50.6 us (15%)
  matrix products  22.8 us (7%)
  blocking collectives  16.6 us (5%)
  between operations  16 us (5%)
  starting transfers between devices  4.77 us (1%)
    psum x1, waiting for transfers between devices, per_device(): lax.psum(jnp.sum(prognostic_vector, axis=0), 'mem') / sample_tally_overall  41.8 us
    psum x1, waiting for transfers between devices, per_device(): posterior_adjustment = lax.psum(inc_part, 'mem')  41 us
    psum x1, waiting for transfers between devices, per_device(): gram_matrix, right_side = lax.psum((gram_part, side_part), 'lon')  36.7 us
    all_gather x1, waiting for transfers between devices, per_device(): all_perts = lax.all_gather(obs_perts, 'mem', axis=0, tiled=True)  35.2 us
    another operation x7, other arithmetic, per_device(): factor = jnp.linalg.cholesky(system)  34.6 us
    another operation x4, other arithmetic, per_device(): weights = jax.scipy.linalg.cho_solve((factor, True), right_side)  20 us
    psum x1, blocking collectives, per_device(): gram_matrix, right_side = lax.psum((gram_part, side_part), 'lon')  16.6 us
    dot_general x1, matrix products, per_device(): jnp.einsum('mk,mlij->klij', w_local, sample_departure, precision=lax.Prec...  13.6 us
  transfers between devices with their start and end apart: 6, of which 4 were waited for; matrix products, arithmetic and copies ran while one was open for 6% of the time, Pallas kernels for 0%

commit v1 on v0

--- a/solution.py
+++ b/solution.py
@@ -1,11 +1,454 @@
+import functools
+
 import jax
 import jax.numpy as jnp
 from jax import lax
+from jax.experimental import pallas as pl
+from jax.experimental.pallas import tpu as pltpu
 from jax.sharding import PartitionSpec as P
 
 KV = 2
 KH = 4
 ADV_STEPS = 2
+MODES = KV * KH
+MESH = pl.DeviceIdType.MESH
+VMEM_LIMIT = 56 * 1024 * 1024
+HIGHEST = lax.Precision.HIGHEST
+
+
+def vmem():
+    return pl.BlockSpec(memory_space=pltpu.VMEM)
+
+
+def smem():
+    return pl.BlockSpec(memory_space=pltpu.SMEM)
+
+
+def greet(peers):
+    barrier = pltpu.get_barrier_semaphore()
+    for peer in peers:
+        pl.semaphore_signal(barrier, inc=1, device_id=peer, device_id_type=MESH)
+    pl.semaphore_wait(barrier, len(peers))
+
+
+def axis_peers(axis, count):
+    me = lax.axis_index(axis)
+    return [{axis: lax.rem(me + d, count)} for d in range(1, count)]
+
+
+def send(src, dst, send_sem, recv_sem, peer):
+    copy = pltpu.make_async_remote_copy(
+        src_ref=src, dst_ref=dst, send_sem=send_sem, recv_sem=recv_sem,
+        device_id=peer, device_id_type=MESH,
+    )
+    copy.start()
+    return copy
+
+
+def advect_kernel(
+    n_lon, n_mem, mem_dev,
+    members, cx, cy, horiz, level, within,
+    prior, mean, obs_prior, obs_horiz,
+    edge_out, edge_in, ext, cx_ext, cy_ext, partial, cols, table, picked, gathered,
+    edge_send, edge_recv, mean_send, mean_recv, obs_send, obs_recv,
+):
+    layers = cx.shape[0]
+    stack, width, lats = members.shape
+    rows = 40
+    halves = lats // 128
+    me = lax.axis_index("lon")
+    me_mem = lax.axis_index("mem")
+    left = {"lon": lax.rem(me + n_lon - 1, n_lon)}
+    right = {"lon": lax.rem(me + 1, n_lon)}
+    others = axis_peers("mem", n_mem)
+
+    for side, (first, second, rim) in enumerate(((0, 1, 0), (width - 2, width - 1, width - 1))):
+        edge_out[side, 0:stack, :] = members[:, first, :]
+        edge_out[side, stack : 2 * stack, :] = members[:, second, :]
+        edge_out[side, 2 * stack : 2 * stack + layers, :] = cx[:, rim, :]
+        edge_out[side, 2 * stack + layers : 2 * stack + 2 * layers, :] = cy[:, rim, :]
+    greet([left, right] + others)
+    to_left = send(edge_out.at[0], edge_in.at[1], edge_send.at[0], edge_recv.at[1], left)
+    to_right = send(edge_out.at[1], edge_in.at[0], edge_send.at[1], edge_recv.at[0], right)
+
+    ext[:, 4 : 4 + width, :] = members[...]
+    cx_ext[:, 4 : 4 + width, :] = cx[...]
+    cy_ext[:, 4 : 4 + width, :] = cy[...]
+    for b in range(2 * KH):
+        for h in range(halves):
+            cols[h, pl.ds(stack + b, width, stride=rows), :] = horiz[
+                b % KH, :, h * 128 : (h + 1) * 128
+            ]
+    to_left.wait_recv()
+    to_right.wait_recv()
+    high = 4 + width
+    ext[:, 2, :] = edge_in[0, 0:stack, :]
+    ext[:, 3, :] = edge_in[0, stack : 2 * stack, :]
+    ext[:, high, :] = edge_in[1, 0:stack, :]
+    ext[:, high + 1, :] = edge_in[1, stack : 2 * stack, :]
+    for side, row in ((0, 3), (1, high)):
+        cx_ext[:, row, :] = edge_in[side, 2 * stack : 2 * stack + layers, :]
+        cy_ext[:, row, :] = edge_in[side, 2 * stack + layers : 2 * stack + 2 * layers, :]
+
+    ext_rows = width + 8
+    lane = lax.broadcasted_iota(jnp.int32, (ext_rows, lats), 1)
+    for l in range(layers):
+        cx_l = cx_ext[l]
+        cy_l = cy_ext[l]
+        east_flow = jnp.maximum(cx_l, 0.0)
+        west_flow = jnp.minimum(cx_l, 0.0)
+        north_flow = jnp.maximum(cy_l, 0.0)
+        south_flow = jnp.minimum(cy_l, 0.0)
+
+        def step(m, total, l=l, flows=(east_flow, west_flow, north_flow, south_flow)):
+            q = ext[m * layers + l]
+            for _ in range(ADV_STEPS):
+                qw = pltpu.roll(q, 1, 0)
+                qe = pltpu.roll(q, ext_rows - 1, 0)
+                qs = jnp.where(lane == 0, 0.0, pltpu.roll(q, 1, 1))
+                qn = jnp.where(lane == lats - 1, 0.0, pltpu.roll(q, lats - 1, 1))
+                r = q - flows[0] * (q - qw)
+                r = r - flows[1] * (qe - q)
+                r = r - flows[2] * (q - qs)
+                q = r - flows[3] * (qn - q)
+            inner = q[4 : 4 + width, :]
+            prior[m * layers + l] = inner
+            for h in range(halves):
+                cols[h, pl.ds(l * mem_dev + m, width, stride=rows), :] = inner[
+                    :, h * 128 : (h + 1) * 128
+                ]
+            return total + inner
+
+        total = lax.fori_loop(0, mem_dev, step, jnp.zeros((width, lats), jnp.float32))
+        partial[me_mem, l] = total
+
+    mean_copies = [
+        send(partial.at[me_mem], partial.at[me_mem], mean_send.at[d], mean_recv.at[d], peer)
+        for d, peer in enumerate(others)
+    ]
+
+    def turn(i, carry):
+        for h in range(halves):
+            block = cols[h, pl.ds(pl.multiple_of(i * rows, 8), rows), :]
+            start = pl.multiple_of(i * lats + h * 128, 128)
+            table[pl.ds(start, 128), 0:rows] = block.T
+        return carry
+
+    lax.fori_loop(0, width, turn, 0)
+
+    slots = within.shape[0]
+    unroll = 16
+
+    def fetch(g, carry):
+        for u in range(unroll):
+            o = g * unroll + u
+            picked[pl.ds(o, 1), :] = table[pl.ds(within[o], 1), :]
+        return carry
+
+    lax.fori_loop(0, slots // unroll, fetch, 0)
+
+    def sort_out(c, carry):
+        start = pl.multiple_of(c * 128, 128)
+        block = picked[pl.ds(start, 128), :].T
+        lev = level[:, pl.ds(start, 128)]
+        value = block[0:mem_dev]
+        for l in range(1, layers):
+            value = jnp.where(lev == l, block[l * mem_dev : (l + 1) * mem_dev], value)
+        gathered[me_mem, :, pl.ds(start, 128)] = value
+        obs_horiz[:, pl.ds(start, 128)] = block[stack : stack + 8]
+        return carry
+
+    lax.fori_loop(0, slots // 128, sort_out, 0)
+    obs_copies = [
+        send(gathered.at[me_mem], gathered.at[me_mem], obs_send.at[d], obs_recv.at[d], peer)
+        for d, peer in enumerate(others)
+    ]
+    for copy in mean_copies:
+        copy.wait_recv()
+    field = partial[0]
+    for g in range(1, n_mem):
+        field = field + partial[g]
+    mean[...] = field / (n_mem * mem_dev)
+    for copy in obs_copies:
+        copy.wait_recv()
+    obs_prior[...] = gathered[...]
+    to_left.wait_send()
+    to_right.wait_send()
+    for copy in mean_copies + obs_copies:
+        copy.wait_send()
+
+
+def gram_kernel(
+    n_lon, n_mem, mem_dev, norm,
+    obs_prior, obs_horiz, level, vert, count, value, var,
+    system,
+    perts, weighted, staged, heard, whole,
+    part_send, part_recv, lon_send, lon_recv, mem_send, mem_recv,
+):
+    slots = level.shape[1]
+    layers = vert.shape[1]
+    total = n_mem * mem_dev
+    local = mem_dev * MODES
+    size = total * MODES
+    me = lax.axis_index("lon")
+    me_mem = lax.axis_index("mem")
+    lon_peers = axis_peers("lon", n_lon)
+    mem_peers = axis_peers("mem", n_mem)
+
+    lev = level[...]
+    states = obs_prior[...].reshape(total, slots)
+    centre = jnp.sum(states, axis=0, keepdims=True) / total
+    slot = lax.broadcasted_iota(jnp.int32, (1, slots), 1)
+    live = jnp.where(slot < count[0], 1.0, 0.0)
+    inv_var = live / var[...]
+    drive = inv_var * (value[...] - centre)
+    scale = live * norm
+    vert_obs = []
+    for a in range(KV):
+        v = jnp.full((1, slots), vert[a, 0])
+        for l in range(1, layers):
+            v = jnp.where(lev == l, vert[a, l], v)
+        vert_obs.append(jnp.broadcast_to(v, (KH, slots)))
+    modes = jnp.concatenate(vert_obs, axis=0) * obs_horiz[...]
+    for g in range(n_mem):
+        for m in range(mem_dev):
+            row = (g * mem_dev + m) * MODES
+            anomaly = obs_prior[g, m : m + 1, :] - centre
+            perts[row : row + MODES, :] = anomaly * modes * scale
+    start = pl.multiple_of(me_mem * local, local)
+    mine = perts[pl.ds(start, local), :]
+    weighted[...] = mine * inv_var
+    gram = lax.dot_general(
+        weighted[...], perts[...], (((1,), (1,)), ((), ())),
+        precision=HIGHEST, preferred_element_type=jnp.float32,
+    )
+    side = jnp.sum(mine * drive, axis=1, keepdims=True)
+    for d in range(n_lon):
+        staged[d, :, 0:size] = gram[d * 8 : (d + 1) * 8]
+        staged[d, :, size : size + 128] = jnp.broadcast_to(side[d * 8 : (d + 1) * 8], (8, 128))
+
+    greet(lon_peers + mem_peers)
+    parts = []
+    for d, peer in enumerate(lon_peers):
+        parts.append(
+            send(staged.at[peer["lon"]], heard.at[me], part_send.at[d], part_recv.at[d], peer)
+        )
+    heard[me] = staged[me]
+    for copy in parts:
+        copy.wait_recv()
+    block = heard[0]
+    for d in range(1, n_lon):
+        block = block + heard[d]
+    whole[me_mem, me] = block
+    spread = [
+        send(whole.at[me_mem, me], whole.at[me_mem, me], lon_send.at[d], lon_recv.at[d], peer)
+        for d, peer in enumerate(lon_peers)
+    ]
+    for copy in spread:
+        copy.wait_recv()
+    across = [
+        send(whole.at[me_mem], whole.at[me_mem], mem_send.at[d], mem_recv.at[d], peer)
+        for d, peer in enumerate(mem_peers)
+    ]
+    for copy in across:
+        copy.wait_recv()
+    system[...] = whole[...].reshape(size, size + 128)
+    for copy in parts + spread + across:
+        copy.wait_send()
+
+
+def solve_kernel(system, weights, work, pivot, strip):
+    size, columns = system.shape
+    row = lax.broadcasted_iota(jnp.int32, (size, columns), 0)
+    col = lax.broadcasted_iota(jnp.int32, (size, columns), 1)
+    work[...] = system[...] + jnp.where(row == col, 1.0, 0.0)
+    for group in range(size // 128):
+        low = group * 128
+        left = columns - low
+
+        def panel(p, carry, low=low, left=left):
+            base = pl.multiple_of(low + p * 8, 8)
+            shift = lax.rem(128 - p * 8, 128)
+            head = pltpu.roll(work[pl.ds(base, 8), low : low + 128], shift, 1)
+            pivot[...] = head
+            strip[...] = work[pl.ds(base, 8), :]
+            a = [
+                [jnp.broadcast_to(pivot[r : r + 1, c : c + 1], (1, 128)) for c in range(8)]
+                for r in range(8)
+            ]
+            rows = [
+                [strip[r : r + 1, low + k * 128 : low + (k + 1) * 128] for k in range(left // 128)]
+                for r in range(8)
+            ]
+            for j in range(8):
+                inv = 1.0 / a[j][j]
+                for c in range(j + 1, 8):
+                    a[j][c] = a[j][c] * inv
+                rows[j] = [x * inv for x in rows[j]]
+                for r in range(8):
+                    if r != j:
+                        f = a[r][j]
+                        for c in range(j + 1, 8):
+                            a[r][c] = a[r][c] - f * a[j][c]
+                        rows[r] = [x - f * y for x, y in zip(rows[r], rows[j])]
+            spread = [[jnp.broadcast_to(x, (8, 128)) for x in rows[r]] for r in range(8)]
+            for i in range(size // 8):
+                block = [work[i * 8 : i * 8 + 8, low + k * 128 : low + (k + 1) * 128] for k in range(left // 128)]
+                lead = pltpu.roll(block[0], shift, 1)
+                for j in range(8):
+                    f = jnp.broadcast_to(lead[:, j : j + 1], (8, 128))
+                    block = [x - f * y for x, y in zip(block, spread[j])]
+                for k in range(left // 128):
+                    work[i * 8 : i * 8 + 8, low + k * 128 : low + (k + 1) * 128] = block[k]
+            for r in range(8):
+                for k in range(left // 128):
+                    strip[r : r + 1, low + k * 128 : low + (k + 1) * 128] = rows[r][k]
+            work[pl.ds(base, 8), low:columns] = strip[:, low:columns]
+            return carry
+
+        lax.fori_loop(0, 16, panel, 0)
+    weights[...] = work[:, size : size + 128]
+
+
+def analysis_kernel(
+    n_mem, mem_dev, norm,
+    weights, prior, mean, horiz, vert,
+    analysis,
+    partial, part_send, part_recv,
+):
+    layers = vert.shape[1]
+    lats = mean.shape[2]
+    me_mem = lax.axis_index("mem")
+    peers = axis_peers("mem", n_mem)
+    for l in range(layers):
+        centre = mean[l]
+        total = jnp.zeros_like(centre)
+        for m in range(mem_dev):
+            start = pl.multiple_of((me_mem * mem_dev + m) * MODES, 8)
+            w = weights[pl.ds(start, MODES), :]
+            mixed = vert[0, l] * w[0:KH] + vert[1, l] * w[KH : 2 * KH]
+            mixed = jnp.concatenate([mixed] * (lats // 128), axis=1)
+            coef = mixed[0:1] * horiz[0]
+            for b in range(1, KH):
+                coef = coef + mixed[b : b + 1] * horiz[b]
+            total = total + coef * (prior[m * layers + l] - centre)
+        partial[me_mem, l] = total
+    greet(peers)
+    copies = [
+        send(partial.at[me_mem], partial.at[me_mem], part_send.at[d], part_recv.at[d], peer)
+        for d, peer in enumerate(peers)
+    ]
+    for copy in copies:
+        copy.wait_recv()
+    field = partial[0]
+    for g in range(1, n_mem):
+        field = field + partial[g]
+    analysis[...] = mean[...] + field * norm
+    for copy in copies:
+        copy.wait_send()
+
+
+def params(collective=None):
+    if collective is None:
+        return pltpu.CompilerParams(vmem_limit_bytes=VMEM_LIMIT)
+    return pltpu.CompilerParams(
+        vmem_limit_bytes=VMEM_LIMIT, collective_id=collective, has_side_effects=True
+    )
+
+
+def fast_device(
+    members, courant_lon, courant_lat, vert_modes, horiz_modes,
+    obs_index, obs_count, obs_value, obs_var,
+):
+    f32 = jnp.float32
+    mem_dev, layers, width, lats = members.shape
+    n_lon = lax.axis_size("lon")
+    n_mem = lax.axis_size("mem")
+    total = mem_dev * n_mem
+    size = total * MODES
+    norm = (total - 1) ** (-0.5)
+    slots = obs_index.shape[0]
+    stack = mem_dev * layers
+    cells = width * lats
+    level = (obs_index // cells).reshape(1, slots)
+    within = obs_index % cells
+    dma = pltpu.SemaphoreType.DMA
+    halves = lats // 128
+    edge_rows = 2 * stack + 2 * layers
+    prior, mean, obs_prior, obs_horiz = pl.pallas_call(
+        functools.partial(advect_kernel, n_lon, n_mem, mem_dev),
+        out_shape=(
+            jax.ShapeDtypeStruct((stack, width, lats), f32),
+            jax.ShapeDtypeStruct((layers, width, lats), f32),
+            jax.ShapeDtypeStruct((n_mem, mem_dev, slots), f32),
+            jax.ShapeDtypeStruct((8, slots), f32),
+        ),
+        in_specs=[vmem()] * 5 + [smem()],
+        out_specs=(vmem(),) * 4,
+        scratch_shapes=[
+            pltpu.VMEM((2, edge_rows, lats), f32),
+            pltpu.VMEM((2, edge_rows, lats), f32),
+            pltpu.VMEM((stack, width + 8, lats), f32),
+            pltpu.VMEM((layers, width + 8, lats), f32),
+            pltpu.VMEM((layers, width + 8, lats), f32),
+            pltpu.VMEM((n_mem, layers, width, lats), f32),
+            pltpu.VMEM((halves, width * 40, 128), f32),
+            pltpu.VMEM((cells, 128), f32),
+            pltpu.VMEM((slots, 128), f32),
+            pltpu.VMEM((n_mem, mem_dev, slots), f32),
+            dma((2,)), dma((2,)),
+            dma((n_mem - 1,)), dma((n_mem - 1,)),
+            dma((n_mem - 1,)), dma((n_mem - 1,)),
+        ],
+        compiler_params=params(1),
+        name="advect",
+    )(members.reshape(stack, width, lats), courant_lon, courant_lat, horiz_modes, level, within)
+    system = pl.pallas_call(
+        functools.partial(gram_kernel, n_lon, n_mem, mem_dev, norm),
+        out_shape=jax.ShapeDtypeStruct((size, size + 128), f32),
+        in_specs=[vmem()] * 3 + [smem()] * 2 + [vmem()] * 2,
+        out_specs=vmem(),
+        scratch_shapes=[
+            pltpu.VMEM((size, slots), f32),
+            pltpu.VMEM((mem_dev * MODES, slots), f32),
+            pltpu.VMEM((n_lon, 8, size + 128), f32),
+            pltpu.VMEM((n_lon, 8, size + 128), f32),
+            pltpu.VMEM((n_mem, n_lon, 8, size + 128), f32),
+            dma((n_lon - 1,)), dma((n_lon - 1,)),
+            dma((n_lon - 1,)), dma((n_lon - 1,)),
+            dma((n_mem - 1,)), dma((n_mem - 1,)),
+        ],
+        compiler_params=params(2),
+        name="gram",
+    )(
+        obs_prior, obs_horiz, level, vert_modes, obs_count,
+        obs_value.reshape(1, slots), obs_var.reshape(1, slots),
+    )
+    weights = pl.pallas_call(
+        solve_kernel,
+        out_shape=jax.ShapeDtypeStruct((size, 128), f32),
+        in_specs=[vmem()],
+        out_specs=vmem(),
+        scratch_shapes=[pltpu.VMEM((size, size + 128), f32),
+            pltpu.VMEM((8, 128), f32),
+            pltpu.VMEM((8, size + 128), f32),
+        ],
+        compiler_params=params(),
+        name="solve",
+    )(system)
+    analysis = pl.pallas_call(
+        functools.partial(analysis_kernel, n_mem, mem_dev, norm),
+        out_shape=jax.ShapeDtypeStruct((layers, width, lats), f32),
+        in_specs=[vmem()] * 4 + [smem()],
+        out_specs=vmem(),
+        scratch_shapes=[
+            pltpu.VMEM((n_mem, layers, width, lats), f32),
+            dma((n_mem - 1,)), dma((n_mem - 1,)),
+        ],
+        compiler_params=params(3),
+        name="analysis",
+    )(weights, prior, mean, horiz_modes, vert_modes)
+    return prior.reshape(members.shape), analysis
 
 
 def padded(block, sides, width):
@@ -110,6 +553,22 @@
     return (prognostic_vector, sample_centroid + posterior_adjustment)
 
 
+def choose(*args):
+    mem_dev, layers, width, lats = args[0].shape
+    n_lon = lax.axis_size("lon")
+    fits = (
+        mem_dev == 8
+        and layers == 4
+        and width % 8 == 0
+        and lats % 128 == 0
+        and args[5].shape[0] % 128 == 0
+        and n_lon > 2
+        and mem_dev * MODES == 8 * n_lon
+        and (mem_dev * lax.axis_size("mem") * MODES) % 128 == 0
+    )
+    return fast_device(*args) if fits else per_device(*args)
+
+
 def solution(mesh):
     placed = (
         P("mem", None, "lon", None),
@@ -123,7 +582,7 @@
         P("lon"),
     )
     return jax.shard_map(
-        per_device,
+        choose,
         mesh=mesh,
         in_specs=placed,
         out_specs=(P("mem", None, "lon", None), P(None, "lon", None)),

time: 333 us -> 154 us (0.46)
  waiting for transfers between devices: 155 us -> 0 us
  Pallas kernels: 0 us -> 149 us
  other arithmetic: 67 us -> 1.31 us
  local copies, waits for them, and re-layouts: 50.6 us -> 1.58 us
  matrix products: 22.8 us -> 0 us
  blocking collectives: 16.6 us -> 0 us
  between operations: 16 us -> 1.33 us
  starting transfers between devices: 4.77 us -> 0 us
    pallas_call x0 -> x4, Pallas kernels: none -> 149 us  [the longest x1 92.4 us: fast_device(): pl.pallas_call(solve_kernel, out_shape=jax.ShapeDtypeStruct((size, 128),...]
    psum x3 -> x0, waiting for transfers between devices: 120 us -> none  [the longest x1 41.8 us: per_device(): lax.psum(jnp.sum(prognostic_vector, axis=0), 'mem') / sample_tally_overall]
    another operation x11 -> x0, other arithmetic: 54.6 us -> none  [the longest x7 34.6 us: per_device(): factor = jnp.linalg.cholesky(system)]
    all_gather x1 -> x0, waiting for transfers between devices: 35.2 us -> none  [per_device(): all_perts = lax.all_gather(obs_perts, 'mem', axis=0, tiled=True)]
    gather x4 -> x0, local copies, waits for them, and re-layouts: 34.7 us -> none  [the longest x1 11.8 us: per_device(): mean_obs = jnp.take(sample_centroid.reshape(-1), obs_index)]
    dot_general x4 -> x0, matrix products: 21.2 us -> none  [the longest x1 13.6 us: per_device(): jnp.einsum('mk,mlij->klij', w_local, sample_departure, precision=lax.Prec...]
    psum x1 -> x0, blocking collectives: 16.6 us -> none  [per_device(): gram_matrix, right_side = lax.psum((gram_part, side_part), 'lon')]
    sub x1 -> x0, local copies, waits for them, and re-layouts: 6.58 us -> none  [per_device(): sample_departure = prognostic_vector - sample_centroid[None]]
  transfers between devices with their start and end apart: 6 -> 0, of which waited for: 4 -> 0; matrix products, arithmetic and copies ran while one was open for 6% -> 0% of each run, Pallas kernels for 0% -> 0%
where the time goes in v1:
time: 154 us
  Pallas kernels  149 us (97%)
  local copies, waits for them, and re-layouts  1.58 us (1%)
    pallas_call x1, Pallas kernels, fast_device(): pl.pallas_call(solve_kernel, out_shape=jax.ShapeDtypeStruct((size, 128),...  92.4 us
    pallas_call x1, Pallas kernels, fast_device(): pl.pallas_call(functools.partial(advect_kernel, n_lon, n_mem, mem_dev), o...  26.6 us
    pallas_call x1, Pallas kernels, fast_device(): pl.pallas_call(functools.partial(gram_kernel, n_lon, n_mem, mem_dev, norm...  20.9 us
    pallas_call x1, Pallas kernels, fast_device(): pl.pallas_call(functools.partial(analysis_kernel, n_mem, mem_dev, norm),...  9.48 us

profile of v1, /device:TPU:0, one launch (start us, length us, event | category | flops | bytes accessed | tf_op | source)
XLA Modules:
  0.0 153.5 jit_solution(11162663614936709813)
XLA Ops:
  1.3 1.3 add_select_fusion
  2.6 26.6 %advect.1 = (f32[32,24,256]{2,1,0:T(8,128)}, f32[4,24,256]{2,1,0:T(8,128)}, f32[4,8,2048]{2,1,0:T(8,128)}, f32[8,2048]{1,0:T(8,128)}) custom-call(f32[32,24,256]{2,1,0:T(8,128)} %bitcast.6, f32[4,24,256]{2,1,0:T(8,128)} %cx.1, f32[4,24,256]{2,1,0:T(8,128)} %cy.1, f32[4,24,256]{2,1,0:T(8,128)} %horiz.3, s32[1,2048]{1,0:T(1,128)} %bitcast.7, ...), custom_call_target="tpu_custom_call" | custom-call | tf_op jit(solution)/shard_map/advect/pallas_call | solution.py:378
  29.1 20.9 %gram.1.system = f32[256,384]{1,0:T(8,128)} custom-call(f32[4,8,2048]{2,1,0:T(8,128)} %get-tuple-element.7.obs_prior, f32[8,2048]{1,0:T(8,128)} %get-tuple-element.8.obs_horiz, s32[1,2048]{1,0:T(1,128)} %bitcast.8, f32[2,4]{1,0:T(2,128)} %vert.3, s32[1]{0:T(128)S(6)} %copy.13.count, f32[1,2048]{1,0:T(1,128)} %bitcast.9, f32[1,2048]{1,0:T(1,128)} %bitcast.10), custom_call_target="tpu_custom_call" | custom-call | tf_op jit(solution)/shard_map/gram/pallas_call | solution.py:406
  50.0 0.0 copy-start
  50.1 92.4 %solve.1.weights = f32[256,128]{1,0:T(8,128)} custom-call(f32[256,384]{1,0:T(8,128)} %gram.1.system), custom_call_target="tpu_custom_call" | custom-call | tf_op jit(solution)/shard_map/solve/pallas_call | solution.py:427
  142.5 9.5 %analysis.1 = f32[4,24,256]{2,1,0:T(8,128)} custom-call(f32[256,128]{1,0:T(8,128)} %solve.1.weights, f32[32,24,256]{2,1,0:T(8,128)} %get-tuple-element.6.prior, f32[4,24,256]{2,1,0:T(8,128)} %get-tuple-element.9.mean, f32[4,24,256]{2,1,0:T(8,128)} %horiz.3, f32[2,4]{1,0:T(2,128)} %vert.3), custom_call_target="tpu_custom_call" | custom-call | tf_op jit(solution)/shard_map/analysis/pallas_call | solution.py:439
  152.0 0.0 copy-done
  152.0 0.0 copy-start.1
  152.0 0.9 copy.14
  152.9 0.0 copy-done.1
  152.9 0.6 copy.15
Async XLA Ops:
  50.0 101.9 %copy-start = (f32[32,24,256]{2,1,0:T(8,128)S(1)}, f32[32,24,256]{2,1,0:T(8,128)}, u32[]{:S(2)}) copy-start(f32[32,24,256]{2,1,0:T(8,128)} %get-tuple-element.6.prior) | copy-start | bytes 2359300
  152.0 0.9 copy-start.1

commit v2 on v1

--- a/solution.py
+++ b/solution.py
@@ -257,56 +257,57 @@
         copy.wait_send()
 
 
-def solve_kernel(system, weights, work, pivot, strip):
+def solve_kernel(system, weights, work):
     size, columns = system.shape
     row = lax.broadcasted_iota(jnp.int32, (size, columns), 0)
     col = lax.broadcasted_iota(jnp.int32, (size, columns), 1)
     work[...] = system[...] + jnp.where(row == col, 1.0, 0.0)
-    for group in range(size // 128):
-        low = group * 128
-        left = columns - low
-
-        def panel(p, carry, low=low, left=left):
-            base = pl.multiple_of(low + p * 8, 8)
-            shift = lax.rem(128 - p * 8, 128)
-            head = pltpu.roll(work[pl.ds(base, 8), low : low + 128], shift, 1)
-            pivot[...] = head
-            strip[...] = work[pl.ds(base, 8), :]
-            a = [
-                [jnp.broadcast_to(pivot[r : r + 1, c : c + 1], (1, 128)) for c in range(8)]
-                for r in range(8)
-            ]
-            rows = [
-                [strip[r : r + 1, low + k * 128 : low + (k + 1) * 128] for k in range(left // 128)]
-                for r in range(8)
-            ]
+    depth = 64
+    tile = (8, 128)
+    sub = lax.broadcasted_iota(jnp.int32, tile, 0)
+    outer = lax.broadcasted_iota(jnp.int32, (size, depth), 0)
+    for top in range(0, size, depth):
+        low = top // 128 * 128
+        pieces = (columns - low) // 128
+        panel = [
+            [work[top + i * 8 : top + i * 8 + 8, low + k * 128 : low + (k + 1) * 128] for k in range(pieces)]
+            for i in range(depth // 8)
+        ]
+        for s in range(depth // 8):
+            lane = top - low + s * 8
+            a = [jnp.broadcast_to(panel[s][0][:, lane + c : lane + c + 1], tile) for c in range(8)]
+            rows = panel[s]
             for j in range(8):
-                inv = 1.0 / a[j][j]
+                inv = 1.0 / jnp.broadcast_to(a[j][j : j + 1], tile)
+                f = a[j]
+
+                def reduce(x, j=j, inv=inv, f=f):
+                    n = jnp.broadcast_to(x[j : j + 1], tile) * inv
+                    return jnp.where(sub == j, n, x - f * n)
+
                 for c in range(j + 1, 8):
-                    a[j][c] = a[j][c] * inv
-                rows[j] = [x * inv for x in rows[j]]
-                for r in range(8):
-                    if r != j:
-                        f = a[r][j]
-                        for c in range(j + 1, 8):
-                            a[r][c] = a[r][c] - f * a[j][c]
-                        rows[r] = [x - f * y for x, y in zip(rows[r], rows[j])]
-            spread = [[jnp.broadcast_to(x, (8, 128)) for x in rows[r]] for r in range(8)]
-            for i in range(size // 8):
-                block = [work[i * 8 : i * 8 + 8, low + k * 128 : low + (k + 1) * 128] for k in range(left // 128)]
-                lead = pltpu.roll(block[0], shift, 1)
+                    a[c] = reduce(a[c])
+                rows = [reduce(x) for x in rows]
+            panel[s] = rows
+            spread = [[jnp.broadcast_to(x[j : j + 1], tile) for x in rows] for j in range(8)]
+            for d in range(1, depth // 8):
+                i = (s + d) % (depth // 8)
+                lead = panel[i][0]
+                block = panel[i]
                 for j in range(8):
-                    f = jnp.broadcast_to(lead[:, j : j + 1], (8, 128))
+                    f = jnp.broadcast_to(lead[:, lane + j : lane + j + 1], tile)
                     block = [x - f * y for x, y in zip(block, spread[j])]
-                for k in range(left // 128):
-                    work[i * 8 : i * 8 + 8, low + k * 128 : low + (k + 1) * 128] = block[k]
-            for r in range(8):
-                for k in range(left // 128):
-                    strip[r : r + 1, low + k * 128 : low + (k + 1) * 128] = rows[r][k]
-            work[pl.ds(base, 8), low:columns] = strip[:, low:columns]
-            return carry
-
-        lax.fori_loop(0, 16, panel, 0)
+                panel[i] = block
+        for i in range(depth // 8):
+            for k in range(pieces):
+                work[top + i * 8 : top + i * 8 + 8, low + k * 128 : low + (k + 1) * 128] = panel[i][k]
+        inside = (outer >= top) & (outer < top + depth)
+        factor = jnp.where(inside, 0.0, work[:, top : top + depth])
+        first = (top + depth) // 128 * 128
+        work[:, first:columns] -= jnp.dot(
+            factor, work[top : top + depth, first:columns],
+            precision=HIGHEST, preferred_element_type=jnp.float32,
+        )
     weights[...] = work[:, size : size + 128]
 
 
@@ -429,10 +430,7 @@
         out_shape=jax.ShapeDtypeStruct((size, 128), f32),
         in_specs=[vmem()],
         out_specs=vmem(),
-        scratch_shapes=[pltpu.VMEM((size, size + 128), f32),
-            pltpu.VMEM((8, 128), f32),
-            pltpu.VMEM((8, size + 128), f32),
-        ],
+        scratch_shapes=[pltpu.VMEM((size, size + 128), f32)],
         compiler_params=params(),
         name="solve",
     )(system)

time: 154 us -> 74.7 us (0.49)
  Pallas kernels: 149 us -> 70.2 us
    pallas_call x1, Pallas kernels: 92.4 us -> 13.3 us  [fast_device(): pl.pallas_call(solve_kernel, out_shape=jax.ShapeDtypeStruct((size, 128),...]
where the time goes in v2:
time: 74.7 us; the launch traced here: 74.4 us
  Pallas kernels  70.2 us (94%)
  local copies, waits for them, and re-layouts  1.58 us (2%)
  between operations  1.33 us (2%)
  other arithmetic  1.31 us (2%)
    pallas_call x1, Pallas kernels, fast_device(): pl.pallas_call(functools.partial(advect_kernel, n_lon, n_mem, mem_dev), o...  26.6 us
    pallas_call x1, Pallas kernels, fast_device(): pl.pallas_call(functools.partial(gram_kernel, n_lon, n_mem, mem_dev, norm...  20.9 us
    pallas_call x1, Pallas kernels, fast_device(): pl.pallas_call(solve_kernel, out_shape=jax.ShapeDtypeStruct((size, 128),...  13.3 us
    pallas_call x1, Pallas kernels, fast_device(): pl.pallas_call(functools.partial(analysis_kernel, n_mem, mem_dev, norm),...  9.48 us
    unnamed x6, local copies, waits for them, and re-layouts  1.58 us

profile of v2, /device:TPU:0, one launch (start us, length us, event | category | flops | bytes accessed | tf_op | source)
XLA Modules:
  0.0 74.4 jit_solution(9673453673316909788)
XLA Ops:
  1.3 1.3 %add_select_fusion = (s32[2048]{0:T(1024)}, s32[2048]{0:T(1024)}) fusion(s32[2048]{0:T(1024)} %param.14), kind=kLoop, calls=%fused_computation | loop fusion | flops 24576 | bytes 24576 | tf_op jit(solution)/shard_map/jit(remainder)/select_n | solution.py:375
  2.6 26.6 %advect.1 = (f32[32,24,256]{2,1,0:T(8,128)}, f32[4,24,256]{2,1,0:T(8,128)}, f32[4,8,2048]{2,1,0:T(8,128)}, f32[8,2048]{1,0:T(8,128)}) custom-call(f32[32,24,256]{2,1,0:T(8,128)} %bitcast.6, f32[4,24,256]{2,1,0:T(8,128)} %cx.1, f32[4,24,256]{2,1,0:T(8,128)} %cy.1, f32[4,24,256]{2,1,0:T(8,128)} %horiz.3, s32[1,2048]{1,0:T(1,128)} %bitcast.7, ...), custom_call_target="tpu_custom_call" | custom-call | tf_op jit(solution)/shard_map/advect/pallas_call | solution.py:379
  29.1 20.9 %gram.1.system = f32[256,384]{1,0:T(8,128)} custom-call(f32[4,8,2048]{2,1,0:T(8,128)} %get-tuple-element.7.obs_prior, f32[8,2048]{1,0:T(8,128)} %get-tuple-element.8.obs_horiz, s32[1,2048]{1,0:T(1,128)} %bitcast.8, f32[2,4]{1,0:T(2,128)} %vert.3, s32[1]{0:T(128)S(6)} %copy.13.count, f32[1,2048]{1,0:T(1,128)} %bitcast.9, f32[1,2048]{1,0:T(1,128)} %bitcast.10), custom_call_target="tpu_custom_call" | custom-call | tf_op jit(solution)/shard_map/gram/pallas_call | solution.py:407
  50.0 0.0 copy-start
  50.1 13.3 %solve.1.weights = f32[256,128]{1,0:T(8,128)} custom-call(f32[256,384]{1,0:T(8,128)} %gram.1.system), custom_call_target="tpu_custom_call" | custom-call | tf_op jit(solution)/shard_map/solve/pallas_call | solution.py:428
  63.3 9.5 %analysis.1 = f32[4,24,256]{2,1,0:T(8,128)} custom-call(f32[256,128]{1,0:T(8,128)} %solve.1.weights, f32[32,24,256]{2,1,0:T(8,128)} %get-tuple-element.6.prior, f32[4,24,256]{2,1,0:T(8,128)} %get-tuple-element.9.mean, f32[4,24,256]{2,1,0:T(8,128)} %horiz.3, f32[2,4]{1,0:T(2,128)} %vert.3), custom_call_target="tpu_custom_call" | custom-call | tf_op jit(solution)/shard_map/analysis/pallas_call | solution.py:437
  72.8 0.0 copy-done
  72.8 0.0 copy-start.1
  72.8 0.9 %copy.14 = f32[8,4,24,256]{3,2,1,0:T(8,128)} copy(f32[8,4,24,256]{3,2,1,0:T(8,128)S(1)} %bitcast.5) | data formatting | bytes 1572864
  73.7 0.0 copy-done.1
  73.8 0.6 copy.15
Async XLA Ops:
  50.0 22.8 %copy-start = (f32[32,24,256]{2,1,0:T(8,128)S(1)}, f32[32,24,256]{2,1,0:T(8,128)}, u32[]{:S(2)}) copy-start(f32[32,24,256]{2,1,0:T(8,128)} %get-tuple-element.6.prior) | copy-start | bytes 2359300
  72.8 0.9 %copy-start.1 = (f32[4,24,256]{2,1,0:T(8,128)S(1)}, f32[4,24,256]{2,1,0:T(8,128)}, u32[]{:S(2)}) copy-start(f32[4,24,256]{2,1,0:T(8,128)} %analysis.1) | copy-start | bytes 294916

commit v3 on v2

--- a/solution.py
+++ b/solution.py
@@ -28,7 +28,7 @@
     barrier = pltpu.get_barrier_semaphore()
     for peer in peers:
         pl.semaphore_signal(barrier, inc=1, device_id=peer, device_id_type=MESH)
-    pl.semaphore_wait(barrier, len(peers))
+    return barrier
 
 
 def axis_peers(axis, count):
@@ -62,12 +62,13 @@
     right = {"lon": lax.rem(me + 1, n_lon)}
     others = axis_peers("mem", n_mem)
 
+    barrier = greet([left, right] + others)
     for side, (first, second, rim) in enumerate(((0, 1, 0), (width - 2, width - 1, width - 1))):
         edge_out[side, 0:stack, :] = members[:, first, :]
         edge_out[side, stack : 2 * stack, :] = members[:, second, :]
         edge_out[side, 2 * stack : 2 * stack + layers, :] = cx[:, rim, :]
         edge_out[side, 2 * stack + layers : 2 * stack + 2 * layers, :] = cy[:, rim, :]
-    greet([left, right] + others)
+    pl.semaphore_wait(barrier, 2 + len(others))
     to_left = send(edge_out.at[0], edge_in.at[1], edge_send.at[0], edge_recv.at[1], left)
     to_right = send(edge_out.at[1], edge_in.at[0], edge_send.at[1], edge_recv.at[0], right)
 
@@ -119,7 +120,9 @@
                 ]
             return total + inner
 
-        total = lax.fori_loop(0, mem_dev, step, jnp.zeros((width, lats), jnp.float32))
+        total = lax.fori_loop(
+            0, mem_dev, step, jnp.zeros((width, lats), jnp.float32), unroll=2
+        )
         partial[me_mem, l] = total
 
     mean_copies = [
@@ -127,25 +130,26 @@
         for d, peer in enumerate(others)
     ]
 
-    def turn(i, carry):
-        for h in range(halves):
-            block = cols[h, pl.ds(pl.multiple_of(i * rows, 8), rows), :]
-            start = pl.multiple_of(i * lats + h * 128, 128)
-            table[pl.ds(start, 128), 0:rows] = block.T
+    def turn(g, carry):
+        for u in range(4):
+            i = g * 4 + u
+            blocks = [cols[h, pl.ds(pl.multiple_of(i * rows, 8), rows), :].T for h in range(halves)]
+            for h in range(halves):
+                table[pl.ds(pl.multiple_of(i * lats + h * 128, 128), 128), 0:rows] = blocks[h]
         return carry
 
-    lax.fori_loop(0, width, turn, 0)
+    lax.fori_loop(0, width // 4, turn, 0)
 
     slots = within.shape[0]
-    unroll = 16
+    unroll = 32
+    chunks = obs_send.shape[0]
+    chunk = slots // chunks
 
     def fetch(g, carry):
+        found = [table[pl.ds(within[g * unroll + u], 1), :] for u in range(unroll)]
         for u in range(unroll):
-            o = g * unroll + u
-            picked[pl.ds(o, 1), :] = table[pl.ds(within[o], 1), :]
+            picked[pl.ds(g * unroll + u, 1), :] = found[u]
         return carry
-
-    lax.fori_loop(0, slots // unroll, fetch, 0)
 
     def sort_out(c, carry):
         start = pl.multiple_of(c * 128, 128)
@@ -158,11 +162,13 @@
         obs_horiz[:, pl.ds(start, 128)] = block[stack : stack + 8]
         return carry
 
-    lax.fori_loop(0, slots // 128, sort_out, 0)
-    obs_copies = [
-        send(gathered.at[me_mem], gathered.at[me_mem], obs_send.at[d], obs_recv.at[d], peer)
-        for d, peer in enumerate(others)
-    ]
+    obs_copies = []
+    for c in range(chunks):
+        lax.fori_loop(c * chunk // unroll, (c + 1) * chunk // unroll, fetch, 0)
+        lax.fori_loop(c * chunk // 128, (c + 1) * chunk // 128, sort_out, 0, unroll=True)
+        piece = gathered.at[me_mem, :, pl.ds(c * chunk, chunk)]
+        for d, peer in enumerate(others):
+            obs_copies.append(send(piece, piece, obs_send.at[c, d], obs_recv.at[c, d], peer))
     for copy in mean_copies:
         copy.wait_recv()
     field = partial[0]
@@ -195,6 +201,7 @@
     lon_peers = axis_peers("lon", n_lon)
     mem_peers = axis_peers("mem", n_mem)
 
+    barrier = greet(lon_peers + mem_peers)
     lev = level[...]
     states = obs_prior[...].reshape(total, slots)
     centre = jnp.sum(states, axis=0, keepdims=True) / total
@@ -227,7 +234,7 @@
         staged[d, :, 0:size] = gram[d * 8 : (d + 1) * 8]
         staged[d, :, size : size + 128] = jnp.broadcast_to(side[d * 8 : (d + 1) * 8], (8, 128))
 
-    greet(lon_peers + mem_peers)
+    pl.semaphore_wait(barrier, len(lon_peers) + len(mem_peers))
     parts = []
     for d, peer in enumerate(lon_peers):
         parts.append(
@@ -257,8 +264,10 @@
         copy.wait_send()
 
 
-def solve_kernel(system, weights, work):
+def solve_kernel(system, prior, weights, prior_out, work, copy_sem):
     size, columns = system.shape
+    keep = pltpu.make_async_copy(prior, prior_out, copy_sem)
+    keep.start()
     row = lax.broadcasted_iota(jnp.int32, (size, columns), 0)
     col = lax.broadcasted_iota(jnp.int32, (size, columns), 1)
     work[...] = system[...] + jnp.where(row == col, 1.0, 0.0)
@@ -309,6 +318,7 @@
             precision=HIGHEST, preferred_element_type=jnp.float32,
         )
     weights[...] = work[:, size : size + 128]
+    keep.wait()
 
 
 def analysis_kernel(
@@ -321,6 +331,8 @@
     lats = mean.shape[2]
     me_mem = lax.axis_index("mem")
     peers = axis_peers("mem", n_mem)
+    barrier = greet(peers)
+    copies = []
     for l in range(layers):
         centre = mean[l]
         total = jnp.zeros_like(centre)
@@ -334,17 +346,18 @@
                 coef = coef + mixed[b : b + 1] * horiz[b]
             total = total + coef * (prior[m * layers + l] - centre)
         partial[me_mem, l] = total
-    greet(peers)
-    copies = [
-        send(partial.at[me_mem], partial.at[me_mem], part_send.at[d], part_recv.at[d], peer)
-        for d, peer in enumerate(peers)
-    ]
-    for copy in copies:
-        copy.wait_recv()
-    field = partial[0]
-    for g in range(1, n_mem):
-        field = field + partial[g]
-    analysis[...] = mean[...] + field * norm
+        if l == 0:
+            pl.semaphore_wait(barrier, len(peers))
+        piece = partial.at[me_mem, l]
+        for d, peer in enumerate(peers):
+            copies.append(send(piece, piece, part_send.at[l, d], part_recv.at[l, d], peer))
+    for l in range(layers):
+        for copy in copies[l * len(peers) : (l + 1) * len(peers)]:
+            copy.wait_recv()
+        field = partial[0, l]
+        for g in range(1, n_mem):
+            field = field + partial[g, l]
+        analysis[l] = mean[l] + field * norm
     for copy in copies:
         copy.wait_send()
 
@@ -371,8 +384,9 @@
     slots = obs_index.shape[0]
     stack = mem_dev * layers
     cells = width * lats
-    level = (obs_index // cells).reshape(1, slots)
-    within = obs_index % cells
+    level = sum((obs_index >= l * cells).astype(jnp.int32) for l in range(1, layers))
+    within = obs_index - cells * level
+    level = level.reshape(1, slots)
     dma = pltpu.SemaphoreType.DMA
     halves = lats // 128
     edge_rows = 2 * stack + 2 * layers
@@ -399,7 +413,7 @@
             pltpu.VMEM((n_mem, mem_dev, slots), f32),
             dma((2,)), dma((2,)),
             dma((n_mem - 1,)), dma((n_mem - 1,)),
-            dma((n_mem - 1,)), dma((n_mem - 1,)),
+            dma((4, n_mem - 1)), dma((4, n_mem - 1)),
         ],
         compiler_params=params(1),
         name="advect",
@@ -425,15 +439,19 @@
         obs_prior, obs_horiz, level, vert_modes, obs_count,
         obs_value.reshape(1, slots), obs_var.reshape(1, slots),
     )
-    weights = pl.pallas_call(
+    anywhere = pl.BlockSpec(memory_space=pl.ANY)
+    weights, prior_out = pl.pallas_call(
         solve_kernel,
-        out_shape=jax.ShapeDtypeStruct((size, 128), f32),
-        in_specs=[vmem()],
-        out_specs=vmem(),
-        scratch_shapes=[pltpu.VMEM((size, size + 128), f32)],
+        out_shape=(
+            jax.ShapeDtypeStruct((size, 128), f32),
+            jax.ShapeDtypeStruct(prior.shape, f32),
+        ),
+        in_specs=[vmem(), vmem()],
+        out_specs=(vmem(), anywhere),
+        scratch_shapes=[pltpu.VMEM((size, size + 128), f32), dma],
         compiler_params=params(),
         name="solve",
-    )(system)
+    )(system, prior)
     analysis = pl.pallas_call(
         functools.partial(analysis_kernel, n_mem, mem_dev, norm),
         out_shape=jax.ShapeDtypeStruct((layers, width, lats), f32),
@@ -441,12 +459,12 @@
         out_specs=vmem(),
         scratch_shapes=[
             pltpu.VMEM((n_mem, layers, width, lats), f32),
-            dma((n_mem - 1,)), dma((n_mem - 1,)),
+            dma((layers, n_mem - 1)), dma((layers, n_mem - 1)),
         ],
         compiler_params=params(3),
         name="analysis",
     )(weights, prior, mean, horiz_modes, vert_modes)
-    return prior.reshape(members.shape), analysis
+    return prior_out.reshape(members.shape), analysis
 
 
 def padded(block, sides, width):
@@ -559,7 +577,7 @@
         and layers == 4
         and width % 8 == 0
         and lats % 128 == 0
-        and args[5].shape[0] % 128 == 0
+        and args[5].shape[0] % 512 == 0
         and n_lon > 2
         and mem_dev * MODES == 8 * n_lon
         and (mem_dev * lax.axis_size("mem") * MODES) % 128 == 0

time: 74.7 us -> 69 us (0.924)
  Pallas kernels: 70.2 us -> 64.5 us
    pallas_call x1, Pallas kernels: 26.6 us -> 22.7 us  [fast_device(): pl.pallas_call(functools.partial(advect_kernel, n_lon, n_mem, mem_dev), o...]
    pallas_call x1, Pallas kernels: 20.9 us -> 18.8 us  [fast_device(): pl.pallas_call(functools.partial(gram_kernel, n_lon, n_mem, mem_dev, norm...]
    select_n x1 -> x0, other arithmetic: 1.31 us -> none  [fast_device(): within = obs_index % cells]
    sub x0 -> x1, other arithmetic: none -> 1.3 us  [fast_device(): within = obs_index - cells * level]
    unnamed x6 -> x1, local copies, waits for them, and re-layouts: 1.58 us -> 1.54 us
where the time goes in v3:
time: 69 us; the launch traced here: 68.7 us
  Pallas kernels  64.5 us (93%)
  local copies, waits for them, and re-layouts  1.54 us (2%)
  between operations  1.31 us (2%)
  other arithmetic  1.3 us (2%)
    pallas_call x1, Pallas kernels, fast_device(): pl.pallas_call(functools.partial(advect_kernel, n_lon, n_mem, mem_dev), o...  22.7 us
    pallas_call x1, Pallas kernels, fast_device(): pl.pallas_call(functools.partial(gram_kernel, n_lon, n_mem, mem_dev, norm...  18.8 us
    pallas_call x1, Pallas kernels, fast_device(): pl.pallas_call(solve_kernel, out_shape=(jax.ShapeDtypeStruct((size, 128),...  13.5 us
    pallas_call x1, Pallas kernels, fast_device(): pl.pallas_call(functools.partial(analysis_kernel, n_mem, mem_dev, norm),...  9.52 us
    unnamed x1, local copies, waits for them, and re-layouts  1.54 us

profile of v3, /device:TPU:0, one launch (start us, length us, event | category | flops | bytes accessed | tf_op | source)
XLA Modules:
  0.0 68.7 jit_solution(2195982711852371918)
XLA Ops:
  1.3 1.3 %multiply_subtract_fusion = (s32[2048]{0:T(1024)}, s32[2048]{0:T(1024)}) fusion(s32[2048]{0:T(1024)} %param.14), kind=kLoop, calls=%fused_computation | loop fusion | flops 20480 | bytes 24576 | tf_op jit(solution)/shard_map/sub | solution.py:388
  2.6 22.7 %advect.1 = (f32[32,24,256]{2,1,0:T(8,128)}, f32[4,24,256]{2,1,0:T(8,128)}, f32[4,8,2048]{2,1,0:T(8,128)}, f32[8,2048]{1,0:T(8,128)}) custom-call(f32[32,24,256]{2,1,0:T(8,128)} %bitcast.5, f32[4,24,256]{2,1,0:T(8,128)} %cx.1, f32[4,24,256]{2,1,0:T(8,128)} %cy.1, f32[4,24,256]{2,1,0:T(8,128)} %horiz.3, s32[1,2048]{1,0:T(1,128)} %bitcast.6, ...), custom_call_target="tpu_custom_call" | custom-call | tf_op jit(solution)/shard_map/advect/pallas_call | solution.py:393
  25.3 18.8 %gram.1.system = f32[256,384]{1,0:T(8,128)} custom-call(f32[4,8,2048]{2,1,0:T(8,128)} %get-tuple-element.8.obs_prior, f32[8,2048]{1,0:T(8,128)} %get-tuple-element.9.obs_horiz, s32[1,2048]{1,0:T(1,128)} %bitcast.7, f32[2,4]{1,0:T(2,128)} %vert.3, s32[1]{0:T(128)S(6)} %copy.12.count, f32[1,2048]{1,0:T(1,128)} %bitcast.8, f32[1,2048]{1,0:T(1,128)} %bitcast.9), custom_call_target="tpu_custom_call" | custom-call | tf_op jit(solution)/shard_map/gram/pallas_call | solution.py:421
  44.1 13.5 %solve.1 = (f32[256,128]{1,0:T(8,128)}, f32[32,24,256]{2,1,0:T(8,128)}) custom-call(f32[256,384]{1,0:T(8,128)} %gram.1.system, f32[32,24,256]{2,1,0:T(8,128)} %get-tuple-element.10.prior), custom_call_target="tpu_custom_call" | custom-call | tf_op jit(solution)/shard_map/solve/pallas_call | solution.py:443
  57.6 9.5 %analysis.1 = f32[4,24,256]{2,1,0:T(8,128)} custom-call(f32[256,128]{1,0:T(8,128)} %get-tuple-element.12.weights, f32[32,24,256]{2,1,0:T(8,128)} %get-tuple-element.10.prior, f32[4,24,256]{2,1,0:T(8,128)} %get-tuple-element.13.mean, f32[4,24,256]{2,1,0:T(8,128)} %horiz.3, f32[2,4]{1,0:T(2,128)} %vert.3), custom_call_target="tpu_custom_call" | custom-call | tf_op jit(solution)/shard_map/analysis/pallas_call | solution.py:455
  67.1 1.5 %copy.13 = f32[4,24,256]{2,1,0:T(8,128)} copy(f32[4,24,256]{2,1,0:T(8,128)} %analysis.1) | data formatting | bytes 196608

commit v4 on v3

--- a/solution.py
+++ b/solution.py
@@ -12,7 +12,7 @@
 ADV_STEPS = 2
 MODES = KV * KH
 MESH = pl.DeviceIdType.MESH
-VMEM_LIMIT = 56 * 1024 * 1024
+VMEM_LIMIT = 20 * 1024 * 1024
 HIGHEST = lax.Precision.HIGHEST
 
 

time: 69 us -> 66 us (0.957)
  Pallas kernels: 64.5 us -> 58.5 us
  local copies, waits for them, and re-layouts: 1.54 us -> 5.12 us
    unnamed x1 -> x17, local copies, waits for them, and re-layouts: 1.54 us -> 5.12 us
    pallas_call x1, Pallas kernels: 13.5 us -> 11.6 us  [fast_device(): pl.pallas_call(solve_kernel, out_shape=(jax.ShapeDtypeStruct((size, 128),...]
    pallas_call x1, Pallas kernels: 22.7 us -> 21.1 us  [fast_device(): pl.pallas_call(functools.partial(advect_kernel, n_lon, n_mem, mem_dev), o...]
    pallas_call x1, Pallas kernels: 9.52 us -> 8.21 us  [fast_device(): pl.pallas_call(functools.partial(analysis_kernel, n_mem, mem_dev, norm),...]
    pallas_call x1, Pallas kernels: 18.8 us -> 17.6 us  [fast_device(): pl.pallas_call(functools.partial(gram_kernel, n_lon, n_mem, mem_dev, norm...]
where the time goes in v4:
time: 66 us; the launch traced here: 65.7 us
  Pallas kernels  58.5 us (89%)
  local copies, waits for them, and re-layouts  5.12 us (8%)
  between operations  1.35 us (2%)
  other arithmetic  0.71 us (1%)
    pallas_call x1, Pallas kernels, fast_device(): pl.pallas_call(functools.partial(advect_kernel, n_lon, n_mem, mem_dev), o...  21.1 us
    pallas_call x1, Pallas kernels, fast_device(): pl.pallas_call(functools.partial(gram_kernel, n_lon, n_mem, mem_dev, norm...  17.6 us
    pallas_call x1, Pallas kernels, fast_device(): pl.pallas_call(solve_kernel, out_shape=(jax.ShapeDtypeStruct((size, 128),...  11.6 us
    pallas_call x1, Pallas kernels, fast_device(): pl.pallas_call(functools.partial(analysis_kernel, n_mem, mem_dev, norm),...  8.21 us
    unnamed x17, local copies, waits for them, and re-layouts  5.12 us

profile of v4, /device:TPU:0, one launch (start us, length us, event | category | flops | bytes accessed | tf_op | source)
XLA Modules:
  0.0 65.7 jit_solution(7293087562052552797)
XLA Ops:
  1.3 0.7 %multiply_subtract_fusion = (s32[2048]{0:T(1024)S(1)}, s32[2048]{0:T(1024)S(1)}) fusion(s32[2048]{0:T(1024)} %param.14), kind=kLoop, calls=%fused_computation | loop fusion | flops 20480 | bytes 24576 | tf_op jit(solution)/shard_map/sub | solution.py:388
  2.0 0.0 copy-start
  2.0 1.1 %copy-done = f32[8,4,24,256]{3,2,1,0:T(8,128)S(1)} copy-done((f32[8,4,24,256]{3,2,1,0:T(8,128)S(1)}, f32[8,4,24,256]{3,2,1,0:T(8,128)}, u32[]{:S(2)}) %copy-start) | copy-done | bytes 786456
  3.1 0.0 copy-start.1
  3.1 0.9 %copy-done.1 = f32[4,24,256]{2,1,0:T(8,128)S(1)} copy-done((f32[4,24,256]{2,1,0:T(8,128)S(1)}, f32[4,24,256]{2,1,0:T(8,128)}, u32[]{:S(2)}) %copy-start.1) | copy-done | bytes 98328
  4.0 0.0 copy-start.3
  4.0 0.9 %copy-done.3 = f32[4,24,256]{2,1,0:T(8,128)S(1)} copy-done((f32[4,24,256]{2,1,0:T(8,128)S(1)}, f32[4,24,256]{2,1,0:T(8,128)}, u32[]{:S(2)}) %copy-start.3) | copy-done | bytes 98328
  4.9 0.0 copy-start.4
  4.9 0.9 %copy-done.4 = f32[4,24,256]{2,1,0:T(8,128)S(1)} copy-done((f32[4,24,256]{2,1,0:T(8,128)S(1)}, f32[4,24,256]{2,1,0:T(8,128)}, u32[]{:S(2)}) %copy-start.4) | copy-done | bytes 98328
  5.8 0.0 copy-start.5
  5.8 0.0 copy-start.6
  5.8 21.1 %advect.1 = (f32[32,24,256]{2,1,0:T(8,128)S(1)}, f32[4,24,256]{2,1,0:T(8,128)S(1)}, f32[4,8,2048]{2,1,0:T(8,128)S(1)}, f32[8,2048]{1,0:T(8,128)S(1)}) custom-call(f32[32,24,256]{2,1,0:T(8,128)S(1)} %bitcast.5, f32[4,24,256]{2,1,0:T(8,128)S(1)} %copy-done.3, f32[4,24,256]{2,1,0:T(8,128)S(1)} %copy-done.4, f32[4,24,256]{2,1,0:T(8,128)S(1)} %copy-done.1, ...), custom_call_target="tpu_custom_call" | custom-call | tf_op jit(solution)/shard_map/advect/pallas_call | solution.py:393
  26.9 0.0 copy-start.7
  26.9 0.0 copy-done.5
  26.9 0.0 copy-done.6
  26.9 0.7 copy-done.7
  27.6 17.6 %gram.1.system = f32[256,384]{1,0:T(8,128)S(1)} custom-call(f32[4,8,2048]{2,1,0:T(8,128)S(1)} %get-tuple-element.8.obs_prior, f32[8,2048]{1,0:T(8,128)S(1)} %get-tuple-element.9.obs_horiz, s32[1,2048]{1,0:T(1,128)S(1)} %bitcast.7, f32[2,4]{1,0:T(2,128)S(1)} %copy-done.7, s32[1]{0:T(128)S(6)} %copy.12.count, f32[1,2048]{1,0:T(1,128)S(1)} %bitcast.8, ...), custom_call_target="tpu_custom_call" | custom-call | tf_op jit(solution)/shard_map/gram/pallas_call | solution.py:421
  45.2 0.0 copy-start.2
  45.2 11.6 %solve.1 = (f32[256,128]{1,0:T(8,128)S(1)}, f32[32,24,256]{2,1,0:T(8,128)}) custom-call(f32[256,384]{1,0:T(8,128)S(1)} %gram.1.system, f32[32,24,256]{2,1,0:T(8,128)S(1)} %get-tuple-element.10.prior), custom_call_target="tpu_custom_call" | custom-call | tf_op jit(solution)/shard_map/solve/pallas_call | solution.py:443
  56.8 0.0 copy-done.2
  56.8 8.2 %analysis.1 = f32[4,24,256]{2,1,0:T(8,128)S(1)} custom-call(f32[256,128]{1,0:T(8,128)S(1)} %get-tuple-element.12.weights, f32[32,24,256]{2,1,0:T(8,128)S(1)} %get-tuple-element.10.prior, f32[4,24,256]{2,1,0:T(8,128)S(1)} %get-tuple-element.13.mean, f32[4,24,256]{2,1,0:T(8,128)S(1)} %copy-done.2, f32[2,4]{1,0:T(2,128)S(1)} %copy-done.7), custom_call_target="tpu_custom_call" | custom-call | tf_op jit(solution)/shard_map/analysis/pallas_call | solution.py:455
  65.0 0.6 copy.13
Async XLA Ops:
  2.0 1.1 %copy-start = (f32[8,4,24,256]{3,2,1,0:T(8,128)S(1)}, f32[8,4,24,256]{3,2,1,0:T(8,128)}, u32[]{:S(2)}) copy-start(f32[8,4,24,256]{3,2,1,0:T(8,128)} %param.9) | copy-start | bytes 2359300
  3.1 0.9 %copy-start.1 = (f32[4,24,256]{2,1,0:T(8,128)S(1)}, f32[4,24,256]{2,1,0:T(8,128)}, u32[]{:S(2)}) copy-start(f32[4,24,256]{2,1,0:T(8,128)} %horiz.3) | copy-start | bytes 294916
  4.0 0.9 %copy-start.3 = (f32[4,24,256]{2,1,0:T(8,128)S(1)}, f32[4,24,256]{2,1,0:T(8,128)}, u32[]{:S(2)}) copy-start(f32[4,24,256]{2,1,0:T(8,128)} %cx.1) | copy-start | bytes 294916
  4.9 0.9 %copy-start.4 = (f32[4,24,256]{2,1,0:T(8,128)S(1)}, f32[4,24,256]{2,1,0:T(8,128)}, u32[]{:S(2)}) copy-start(f32[4,24,256]{2,1,0:T(8,128)} %cy.1) | copy-start | bytes 294916
  5.8 21.1 %copy-start.5 = (f32[2048]{0:T(1024)S(1)}, f32[2048]{0:T(1024)}, u32[]{:S(2)}) copy-start(f32[2048]{0:T(1024)} %param.16) | copy-start | bytes 24580
  5.8 21.1 %copy-start.6 = (f32[2048]{0:T(1024)S(1)}, f32[2048]{0:T(1024)}, u32[]{:S(2)}) copy-start(f32[2048]{0:T(1024)} %param.17) | copy-start | bytes 24580
  26.9 0.7 %copy-start.7 = (f32[2,4]{1,0:T(2,128)S(1)}, f32[2,4]{1,0:T(2,128)}, u32[]{:S(2)}) copy-start(f32[2,4]{1,0:T(2,128)} %vert.3) | copy-start | bytes 100
  45.2 11.6 %copy-start.2 = (f32[4,24,256]{2,1,0:T(8,128)S(1)}, f32[4,24,256]{2,1,0:T(8,128)}, u32[]{:S(2)}) copy-start(f32[4,24,256]{2,1,0:T(8,128)} %horiz.3) | copy-start | bytes 294916

commit v5 on v4

--- a/solution.py
+++ b/solution.py
@@ -121,7 +121,7 @@
             return total + inner
 
         total = lax.fori_loop(
-            0, mem_dev, step, jnp.zeros((width, lats), jnp.float32), unroll=2
+            0, mem_dev, step, jnp.zeros((width, lats), jnp.float32), unroll=4
         )
         partial[me_mem, l] = total
 
@@ -131,14 +131,14 @@
     ]
 
     def turn(g, carry):
-        for u in range(4):
-            i = g * 4 + u
+        for u in range(8):
+            i = g * 8 + u
             blocks = [cols[h, pl.ds(pl.multiple_of(i * rows, 8), rows), :].T for h in range(halves)]
             for h in range(halves):
                 table[pl.ds(pl.multiple_of(i * lats + h * 128, 128), 128), 0:rows] = blocks[h]
         return carry
 
-    lax.fori_loop(0, width // 4, turn, 0)
+    lax.fori_loop(0, width // 8, turn, 0)
 
     slots = within.shape[0]
     unroll = 32

time: 66 us -> 65 us (0.985)
  Pallas kernels: 58.5 us -> 57.5 us
    pallas_call x1, Pallas kernels: 21.1 us -> 20.1 us  [fast_device(): pl.pallas_call(functools.partial(advect_kernel, n_lon, n_mem, mem_dev), o...]
where the time goes in v5:
time: 65 us; the launch traced here: 64.7 us
  Pallas kernels  57.5 us (88%)
  local copies, waits for them, and re-layouts  5.12 us (8%)
  between operations  1.35 us (2%)
  other arithmetic  0.71 us (1%)
    pallas_call x1, Pallas kernels, fast_device(): pl.pallas_call(functools.partial(advect_kernel, n_lon, n_mem, mem_dev), o...  20.1 us
    pallas_call x1, Pallas kernels, fast_device(): pl.pallas_call(functools.partial(gram_kernel, n_lon, n_mem, mem_dev, norm...  17.6 us
    pallas_call x1, Pallas kernels, fast_device(): pl.pallas_call(solve_kernel, out_shape=(jax.ShapeDtypeStruct((size, 128),...  11.6 us
    pallas_call x1, Pallas kernels, fast_device(): pl.pallas_call(functools.partial(analysis_kernel, n_mem, mem_dev, norm),...  8.21 us
    unnamed x17, local copies, waits for them, and re-layouts  5.12 us

profile of v5, /device:TPU:0, one launch (start us, length us, event | category | flops | bytes accessed | tf_op | source)
XLA Modules:
  0.0 64.7 jit_solution(3004139890199570315)
XLA Ops:
  1.3 0.7 %multiply_subtract_fusion = (s32[2048]{0:T(1024)S(1)}, s32[2048]{0:T(1024)S(1)}) fusion(s32[2048]{0:T(1024)} %param.14), kind=kLoop, calls=%fused_computation | loop fusion | flops 20480 | bytes 24576 | tf_op jit(solution)/shard_map/sub | solution.py:388
  2.0 0.0 copy-start
  2.0 1.1 %copy-done = f32[8,4,24,256]{3,2,1,0:T(8,128)S(1)} copy-done((f32[8,4,24,256]{3,2,1,0:T(8,128)S(1)}, f32[8,4,24,256]{3,2,1,0:T(8,128)}, u32[]{:S(2)}) %copy-start) | copy-done | bytes 786456
  3.1 0.0 copy-start.1
  3.1 0.9 %copy-done.1 = f32[4,24,256]{2,1,0:T(8,128)S(1)} copy-done((f32[4,24,256]{2,1,0:T(8,128)S(1)}, f32[4,24,256]{2,1,0:T(8,128)}, u32[]{:S(2)}) %copy-start.1) | copy-done | bytes 98328
  4.0 0.0 copy-start.3
  4.0 0.9 %copy-done.3 = f32[4,24,256]{2,1,0:T(8,128)S(1)} copy-done((f32[4,24,256]{2,1,0:T(8,128)S(1)}, f32[4,24,256]{2,1,0:T(8,128)}, u32[]{:S(2)}) %copy-start.3) | copy-done | bytes 98328
  4.9 0.0 copy-start.4
  4.9 0.9 %copy-done.4 = f32[4,24,256]{2,1,0:T(8,128)S(1)} copy-done((f32[4,24,256]{2,1,0:T(8,128)S(1)}, f32[4,24,256]{2,1,0:T(8,128)}, u32[]{:S(2)}) %copy-start.4) | copy-done | bytes 98328
  5.8 0.0 copy-start.5
  5.8 0.0 copy-start.6
  5.8 20.1 %advect.1 = (f32[32,24,256]{2,1,0:T(8,128)S(1)}, f32[4,24,256]{2,1,0:T(8,128)S(1)}, f32[4,8,2048]{2,1,0:T(8,128)S(1)}, f32[8,2048]{1,0:T(8,128)S(1)}) custom-call(f32[32,24,256]{2,1,0:T(8,128)S(1)} %bitcast.5, f32[4,24,256]{2,1,0:T(8,128)S(1)} %copy-done.3, f32[4,24,256]{2,1,0:T(8,128)S(1)} %copy-done.4, f32[4,24,256]{2,1,0:T(8,128)S(1)} %copy-done.1, ...), custom_call_target="tpu_custom_call" | custom-call | tf_op jit(solution)/shard_map/advect/pallas_call | solution.py:393
  25.9 0.0 copy-start.7
  25.9 0.0 copy-done.5
  25.9 0.0 copy-done.6
  25.9 0.7 %copy-done.7 = f32[2,4]{1,0:T(2,128)S(1)} copy-done((f32[2,4]{1,0:T(2,128)S(1)}, f32[2,4]{1,0:T(2,128)}, u32[]{:S(2)}) %copy-start.7) | copy-done | bytes 56
  26.5 17.6 %gram.1.system = f32[256,384]{1,0:T(8,128)S(1)} custom-call(f32[4,8,2048]{2,1,0:T(8,128)S(1)} %get-tuple-element.8.obs_prior, f32[8,2048]{1,0:T(8,128)S(1)} %get-tuple-element.9.obs_horiz, s32[1,2048]{1,0:T(1,128)S(1)} %bitcast.7, f32[2,4]{1,0:T(2,128)S(1)} %copy-done.7, s32[1]{0:T(128)S(6)} %copy.12.count, f32[1,2048]{1,0:T(1,128)S(1)} %bitcast.8, ...), custom_call_target="tpu_custom_call" | custom-call | tf_op jit(solution)/shard_map/gram/pallas_call | solution.py:421
  44.2 0.0 copy-start.2
  44.2 11.6 %solve.1 = (f32[256,128]{1,0:T(8,128)S(1)}, f32[32,24,256]{2,1,0:T(8,128)}) custom-call(f32[256,384]{1,0:T(8,128)S(1)} %gram.1.system, f32[32,24,256]{2,1,0:T(8,128)S(1)} %get-tuple-element.10.prior), custom_call_target="tpu_custom_call" | custom-call | tf_op jit(solution)/shard_map/solve/pallas_call | solution.py:443
  55.8 0.0 copy-done.2
  55.8 8.2 %analysis.1 = f32[4,24,256]{2,1,0:T(8,128)S(1)} custom-call(f32[256,128]{1,0:T(8,128)S(1)} %get-tuple-element.12.weights, f32[32,24,256]{2,1,0:T(8,128)S(1)} %get-tuple-element.10.prior, f32[4,24,256]{2,1,0:T(8,128)S(1)} %get-tuple-element.13.mean, f32[4,24,256]{2,1,0:T(8,128)S(1)} %copy-done.2, f32[2,4]{1,0:T(2,128)S(1)} %copy-done.7), custom_call_target="tpu_custom_call" | custom-call | tf_op jit(solution)/shard_map/analysis/pallas_call | solution.py:455
  64.0 0.6 copy.13
Async XLA Ops:
  2.0 1.1 %copy-start = (f32[8,4,24,256]{3,2,1,0:T(8,128)S(1)}, f32[8,4,24,256]{3,2,1,0:T(8,128)}, u32[]{:S(2)}) copy-start(f32[8,4,24,256]{3,2,1,0:T(8,128)} %param.9) | copy-start | bytes 2359300
  3.1 0.9 %copy-start.1 = (f32[4,24,256]{2,1,0:T(8,128)S(1)}, f32[4,24,256]{2,1,0:T(8,128)}, u32[]{:S(2)}) copy-start(f32[4,24,256]{2,1,0:T(8,128)} %horiz.3) | copy-start | bytes 294916
  4.0 0.9 %copy-start.3 = (f32[4,24,256]{2,1,0:T(8,128)S(1)}, f32[4,24,256]{2,1,0:T(8,128)}, u32[]{:S(2)}) copy-start(f32[4,24,256]{2,1,0:T(8,128)} %cx.1) | copy-start | bytes 294916
  4.9 0.9 %copy-start.4 = (f32[4,24,256]{2,1,0:T(8,128)S(1)}, f32[4,24,256]{2,1,0:T(8,128)}, u32[]{:S(2)}) copy-start(f32[4,24,256]{2,1,0:T(8,128)} %cy.1) | copy-start | bytes 294916
  5.8 20.1 %copy-start.5 = (f32[2048]{0:T(1024)S(1)}, f32[2048]{0:T(1024)}, u32[]{:S(2)}) copy-start(f32[2048]{0:T(1024)} %param.16) | copy-start | bytes 24580
  5.8 20.1 %copy-start.6 = (f32[2048]{0:T(1024)S(1)}, f32[2048]{0:T(1024)}, u32[]{:S(2)}) copy-start(f32[2048]{0:T(1024)} %param.17) | copy-start | bytes 24580
  25.9 0.7 %copy-start.7 = (f32[2,4]{1,0:T(2,128)S(1)}, f32[2,4]{1,0:T(2,128)}, u32[]{:S(2)}) copy-start(f32[2,4]{1,0:T(2,128)} %vert.3) | copy-start | bytes 100
  44.2 11.6 %copy-start.2 = (f32[4,24,256]{2,1,0:T(8,128)S(1)}, f32[4,24,256]{2,1,0:T(8,128)}, u32[]{:S(2)}) copy-start(f32[4,24,256]{2,1,0:T(8,128)} %horiz.3) | copy-start | bytes 294916
